TPU v7x, 512 devices: a whole 4x8x8 slice. The times are simulated.
512 devices in a mesh: coil: 32 (over x, y), slab: 16 (over z, core).
Axes of the slice: x: 4, y: 8, z: 8, core: 2. Of those that a mesh axis runs over, the one named last changes fastest.
Arguments:
- adjoint_data: float32 [16, 192, 384], P('slab', 'coil'), may hold values from -80 to 80
- denoised: float32 [16, 192, 384], P('slab', 'coil'), may hold values from -8 to 8, as said below
- sensitivity: float32 [32, 16, 192, 384], P('coil', 'slab'), may hold values from -2 to 2, as said below
- kernel: float32 [16, 384, 384], P(None, 'slab'), may hold values from 0.1 to 2, as said below
- conv_in: bfloat16 [54, 64], replicated, may hold values from -0.875 to 0.875
- conv_mid: bfloat16 [1728, 64], replicated, may hold values from -0.15625 to 0.15625
- conv_out: bfloat16 [1728, 2], replicated, may hold values from -0.15625 to 0.15625
Outputs:
- solution: float32 [16, 192, 384], P('slab', 'coil')
- refined: float32 [16, 192, 384], P('slab', 'coil')
Inputs may be any that keep to these rules, and one draw needn't show every extreme that they name: `denoised`: real and imaginary parts of the previous cascade's image. `sensitivity`: real and imaginary parts of the coil maps. Positive kernel values.
All inputs are finite; a program needn't handle non-finite values.
Results may differ from a plain program's by a relative error of at most 0.0023.
Values may be sent and summed in bfloat16 or wider, within the bound.
A program may use at most 64 MiB of HBM per device.

v0:
```python
import math
import jax
import jax.numpy as jnp
from jax import lax
from jax.sharding import PartitionSpec as P

ITERS = 2
reg_weight = 0.5
highest = lax.Precision.HIGHEST


def with_halo(cells, sides, width):
    for axis, dim in sides:
        count = lax.axis_size(axis)
        ends = count - 1
        head = lax.slice_in_dim(cells, 0, width, axis=dim)
        tail = lax.slice_in_dim(cells, cells.shape[dim] - width, cells.shape[dim], axis=dim)
        cells = jnp.concatenate(
            [
                lax.ppermute(tail, axis, [(i, (i + 1) % count) for i in range(ends)]),
                cells,
                lax.ppermute(head, axis, [((i + 1) % count, i) for i in range(ends)]),
            ],
            axis=dim,
        )
    return cells


def dft_tables(out_len, in_len, length, inverse):
    out_index = lax.broadcasted_iota(jnp.int32, (out_len, in_len), 0)
    in_index = lax.broadcasted_iota(jnp.int32, (out_len, in_len), 1)
    phases = (out_index * in_index % length).astype(jnp.float32) * (2.0 * math.pi / length)
    if inverse:
        return (jnp.cos(phases) / length, jnp.sin(phases) / length)
    return (jnp.cos(phases), -jnp.sin(phases))


def block_matrix(tables):
    cos_table = tables[0]
    sin_table = tables[1]
    upper = jnp.concatenate([cos_table.T, sin_table.T], axis=1)
    lower = jnp.concatenate([-sin_table.T, cos_table.T], axis=1)
    return jnp.concatenate([upper, lower], axis=0)


def along_axis(values, tables, einsum_form):
    half_len = values.shape[-1] // 2
    real_part = jnp.einsum(einsum_form, tables[0], values, precision=highest)
    imag_part = jnp.einsum(einsum_form, tables[1], values, precision=highest)
    return jnp.concatenate(
        [
            real_part[..., :half_len] - imag_part[..., half_len:],
            real_part[..., half_len:] + imag_part[..., :half_len],
        ],
        axis=-1,
    )


def complex_product(factor_one, factor_two):
    half_len = factor_one.shape[-1] // 2
    real_one = factor_one[..., :half_len]
    imag_one = factor_one[..., half_len:]
    real_two = factor_two[..., :half_len]
    imag_two = factor_two[..., half_len:]
    return jnp.concatenate(
        [real_one * real_two - imag_one * imag_two, real_one * imag_two + imag_one * real_two],
        axis=-1,
    )


def conj_product(factor_one, factor_two):
    half_len = factor_one.shape[-1] // 2
    real_one = factor_one[..., :half_len]
    imag_one = factor_one[..., half_len:]
    real_two = factor_two[..., :half_len]
    imag_two = factor_two[..., half_len:]
    return jnp.concatenate(
        [real_one * real_two + imag_one * imag_two, real_one * imag_two - imag_one * real_two],
        axis=-1,
    )


def convolve(features, weights, in_channels):
    padded = with_halo(features, (("coil", 1), ("slab", 0)), 1)
    depth_here = features.shape[0]
    rows_here = features.shape[1]
    side_len = features.shape[2] // in_channels
    padded_cube = padded.reshape(depth_here + 2, rows_here + 2, side_len, in_channels)
    padded_cube = jnp.pad(padded_cube, ((0, 0), (0, 0), (1, 1), (0, 0)))
    width_taps = 9 * in_channels
    running = None
    for shift_z in range(3):
        tap_list = [
            padded_cube[
                shift_z : shift_z + depth_here,
                shift_x : shift_x + rows_here,
                shift_y : shift_y + side_len,
                :,
            ]
            for shift_x in range(3)
            for shift_y in range(3)
        ]
        patches = jnp.concatenate(tap_list, axis=-1).reshape(-1, width_taps)
        partial_sum = jnp.dot(
            patches,
            weights[shift_z * width_taps : (shift_z + 1) * width_taps],
            preferred_element_type=jnp.float32,
        )
        running = partial_sum if shift_z == 0 else running + partial_sum
    return running


def shards(adjoint_data, denoised, sensitivity, kernel, conv_in, conv_mid, conv_out):
    side_len = sensitivity.shape[2]
    depth_len = kernel.shape[0]
    grid_len = kernel.shape[2]
    fwd_plane = dft_tables(grid_len, side_len, grid_len, False)
    inv_plane = dft_tables(side_len, grid_len, grid_len, True)
    fwd_depth = dft_tables(depth_len, depth_len, depth_len, False)
    inv_depth = dft_tables(depth_len, depth_len, depth_len, True)
    fwd_last = block_matrix(fwd_plane)
    inv_last = block_matrix(inv_plane)

    def total_squares(residual):
        return lax.psum(jnp.sum(residual * residual), ("coil", "slab"))

    right_side = adjoint_data + reg_weight * denoised
    solution = jnp.zeros_like(right_side)
    residual = right_side
    direction = right_side
    norm_now = total_squares(residual)
    for iteration in range(ITERS):
        products = complex_product(
            sensitivity, lax.all_gather(direction, "coil", axis=1, tiled=True)[None]
        )
        products = jnp.matmul(products, fwd_last, precision=highest)
        spread = along_axis(products, fwd_plane, "kn,cznw->czkw")
        apply_pencil = lax.all_to_all(spread, "slab", split_axis=2, concat_axis=1, tiled=True)
        spectrum = along_axis(apply_pencil, fwd_depth, "kn,cnxw->ckxw")
        shape_now = spectrum.shape
        split_form = spectrum.reshape(shape_now[0], shape_now[1], shape_now[2], 2, grid_len)
        weighted = split_form * kernel[None, :, :, None, :]
        returned = along_axis(weighted.reshape(shape_now), inv_depth, "kn,cnxw->ckxw")
        slab_back = lax.all_to_all(returned, "slab", split_axis=1, concat_axis=2, tiled=True)
        image_back = along_axis(slab_back, inv_plane, "kn,cznw->czkw")
        image_back = jnp.matmul(image_back, inv_last, precision=highest)
        coil_sum = jnp.sum(conj_product(sensitivity, image_back), axis=0)
        summed = lax.psum_scatter(coil_sum, "coil", scatter_dimension=1, tiled=True)
        image_out = summed + reg_weight * direction
        local_curv = jnp.sum(direction * image_out)
        image_out, local_curv = (image_out, local_curv)
        curvature = lax.psum(local_curv, ("coil", "slab"))
        step_size = norm_now / curvature
        solution = solution + step_size * direction
        if iteration + 1 < ITERS:
            residual = residual - step_size * image_out
            norm_next = total_squares(residual)
            direction = residual + norm_next / norm_now * direction
            norm_now = norm_next
    depth_here = solution.shape[0]
    rows_here = solution.shape[1]
    channels = jnp.stack([solution[..., :side_len], solution[..., side_len:]], axis=-1).astype(
        jnp.bfloat16
    )
    first_map = convolve(channels.reshape(depth_here, rows_here, 2 * side_len), conv_in, 2)
    hidden_count = conv_mid.shape[1]
    hidden_one = (
        jax.nn.relu(first_map)
        .astype(jnp.bfloat16)
        .reshape(depth_here, rows_here, side_len * hidden_count)
    )
    second_map = convolve(hidden_one, conv_mid, hidden_count)
    hidden_two = (
        jax.nn.relu(second_map)
        .astype(jnp.bfloat16)
        .reshape(depth_here, rows_here, side_len * hidden_count)
    )
    third_map = convolve(hidden_two, conv_out, hidden_count).reshape(
        depth_here, rows_here, side_len, 2
    )
    refined = solution + jnp.concatenate([third_map[..., 0], third_map[..., 1]], axis=-1)
    return (solution, refined)


def solution(mesh):
    placed = (
        P("slab", "coil", None),
        P("slab", "coil", None),
        P("coil", "slab", None, None),
        P(None, "slab", None),
        P(),
        P(),
        P(),
    )
    return jax.shard_map(
        shards,
        mesh=mesh,
        in_specs=placed,
        out_specs=(P("slab", "coil", None), P("slab", "coil", None)),
        check_vma=False,
    )
```

profile of v0, /device:TPU:249, one launch (start us, length us, event | category | flops | bytes accessed | tf_op | source)
XLA Modules:
  0.0 1028.2 jit_solution(9897725327793448658)
XLA Ops:
  10.4 37.1 %all_gather.6 = f32[1,192,384]{2,0,1:T(1,128)S(1)} all-gather(f32[1,6,384]{2,0,1:T(1,128)S(1)} %copy.111), channel_id=1, replica_groups=mesh['coil'=32,'slab'=16] {'coil'}, dimensions={1}, use_global_device_ids=true | all-gather | bytes 304128 | tf_op jit(solution)/shard_map/all_gather | solution.py:134
  48.9 4.0 convolution_bitcast_fusion.10
  52.9 4.0 convolution_bitcast_fusion.11
  57.1 2.7 copy.112
  59.8 21.2 %all-to-all-start = ((f32[1,1,384,768]{3,1,0,2:T(1,128)}), f32[1,1,384,768]{3,1,0,2:T(1,128)S(1)}, u32[]{:S(2)}, u32[]{:S(2)}) async-start(f32[1,1,384,768]{3,1,0,2:T(1,128)} %copy.112), calls=%async_computation | async-start | bytes 2359296 | tf_op jit(solution)/shard_map/all_to_all | solution.py:138
  82.9 2.2 mul.250
  85.1 25.0 %all-to-all-done = f32[1,1,384,768]{3,1,0,2:T(1,128)S(1)} async-done(((f32[1,1,384,768]{3,1,0,2:T(1,128)}), f32[1,1,384,768]{3,1,0,2:T(1,128)S(1)}, u32[]{:S(2)}, u32[]{:S(2)}) %all-to-all-start) | async-done | bytes 1179680 | tf_op jit(solution)/shard_map/all_to_all | solution.py:138
  117.6 5.2 all-to-all-start.1
  124.5 2.4 fusion.25
  127.0 24.9 %all-to-all-done.1 = f32[1,16,24,768]{3,2,0,1:T(8,128)S(1)} async-done(((f32[1,16,24,768]{3,2,0,1:T(8,128)}), f32[1,16,24,768]{3,2,0,1:T(8,128)S(1)}, u32[]{:S(2)}, u32[]{:S(2)}) %all-to-all-start.1) | async-done | bytes 1179680 | tf_op jit(solution)/shard_map/all_to_all | solution.py:144
  151.8 2.3 convolution_bitcast_fusion.14
  154.1 2.3 convolution_bitcast_fusion.15
  162.2 145.9 %all-reduce.9.cloned.1.call-done = f32[1,192,384]{2,0,1:T(1,128)} async-done(((f32[1,192,384]{2,0,1:T(1,128)}), f32[1,192,384]{2,0,1:T(1,128)}) %all-reduce.9.cloned.1.call-update) | async-done | bytes 294928
  309.4 99.0 %all-reduce.5 = (f32[]{:T(128)}, f32[]{:T(128)}) all-reduce(f32[]{:T(128)} %get-tuple-element.13, f32[]{:T(128)} %get-tuple-element.12), channel_id=1, replica_groups=mesh['coil'=32,'slab'=16] {'coil','slab'}, use_global_device_ids=true, to_apply=%region_1.2 | all-reduce | flops 2 | bytes 16 | tf_op jit(solution)/shard_map/psum | solution.py:125
  410.4 94.7 %psum.30 = f32[]{:T(128)} all-reduce(f32[]{:T(128)} %multiply_reduce_fusion), channel_id=1, replica_groups=mesh['coil'=32,'slab'=16] {'coil','slab'}, use_global_device_ids=true, to_apply=%region_6.7 | all-reduce | flops 1 | bytes 8 | tf_op jit(solution)/shard_map/psum | solution.py:125
  506.5 37.2 %all_gather.7 = f32[1,192,384]{2,0,1:T(1,128)S(1)} all-gather(f32[1,6,384]{2,0,1:T(1,128)S(1)} %copy.119), channel_id=1, replica_groups=mesh['coil'=32,'slab'=16] {'coil'}, dimensions={1}, use_global_device_ids=true | all-gather | bytes 304128 | tf_op jit(solution)/shard_map/all_gather | solution.py:134
  545.1 4.0 convolution_bitcast_fusion.8
  549.1 4.0 convolution_bitcast_fusion.9
  553.3 2.7 copy.120
  556.0 47.3 %all_to_all.16 = f32[1,1,384,768]{3,1,0,2:T(1,128)S(1)} all-to-all(f32[1,1,384,768]{3,1,0,2:T(1,128)} %copy.120), channel_id=1, replica_groups=mesh['coil'=32,'slab'=16] {'slab'}, dimensions={2} | all-to-all | bytes 2359296 | tf_op jit(solution)/shard_map/all_to_all | solution.py:138
  609.9 34.2 %all_to_all.17 = f32[1,16,24,768]{3,2,0,1:T(8,128)S(1)} all-to-all(f32[1,16,24,768]{3,2,0,1:T(8,128)S(1)} %copy.123), channel_id=1, replica_groups=mesh['coil'=32,'slab'=16] {'slab'}, dimensions={1} | all-to-all | bytes 2359296 | tf_op jit(solution)/shard_map/all_to_all | solution.py:144
  644.1 2.3 convolution_bitcast_fusion.12
  646.4 2.3 convolution_bitcast_fusion.13
  652.4 148.8 %all-reduce.11.cloned.1.call-done = f32[1,192,384]{2,0,1:T(1,128)} async-done(((f32[1,192,384]{2,0,1:T(1,128)}), f32[1,192,384]{2,0,1:T(1,128)}) %all-reduce.11.cloned.1.call-update) | async-done | bytes 294928
  802.5 98.9 %psum.31 = f32[]{:T(128)} all-reduce(f32[]{:T(128)} %fusion.74), channel_id=1, replica_groups=mesh['coil'=32,'slab'=16] {'coil','slab'}, use_global_device_ids=true, to_apply=%region_9.10 | all-reduce | flops 1 | bytes 8 | tf_op jit(solution)/shard_map/psum | solution.py:152
  903.1 5.1 collective-permute-start
  910.3 5.3 collective-permute-done.1
  915.8 4.0 collective-permute-start.3
  919.8 3.5 collective-permute-start.2
  927.2 4.2 concatenate.143
  940.3 3.4 collective-permute-start.5
  943.7 3.6 collective-permute-done.5
  947.4 4.0 collective-permute-start.7
  951.4 4.7 collective-permute-start.6
  962.9 2.0 pad_slice_fusion.19
  964.8 3.1 concatenate.146
  967.9 2.2 fusion.71
  970.1 2.7 concatenate.147
  972.8 2.4 convolution_add_fusion.1
  975.2 2.9 concatenate.148
  982.1 3.4 collective-permute-start.9
  985.5 4.0 collective-permute-done.9
  989.6 2.7 collective-permute-start.11
  992.3 5.5 collective-permute-start.10
  1004.9 2.0 pad_slice_fusion.1
  1006.8 3.1 concatenate.151
  1011.7 2.7 concatenate.152
  1016.2 2.9 concatenate.153
  (144 shorter events, 74.5 us)
Async XLA Ops:
  7.2 40.4 %copy-start = (f32[1,1,192,384]{3,2,1,0:T(8,128)S(1)}, f32[1,1,192,384]{3,2,1,0:T(8,128)}, u32[]{:S(2)}) copy-start(f32[1,1,192,384]{3,2,1,0:T(8,128)} %param.9) | copy-start | bytes 884740
  8.3 39.4 %copy-start.5 = (f32[192,384]{1,0:T(8,128)}, f32[192,384]{1,0:T(8,128)S(1)}, u32[]{:S(2)}) copy-start(f32[192,384]{1,0:T(8,128)S(1)} %fusion.66) | copy-start | bytes 884740
  9.5 39.4 %copy-start.7 = (f32[192,384]{1,0:T(8,128)}, f32[192,384]{1,0:T(8,128)S(1)}, u32[]{:S(2)}) copy-start(f32[192,384]{1,0:T(8,128)S(1)} %get-tuple-element.133) | copy-start | bytes 884740
  9.5 39.4 %copy-start.9 = (f32[192,384]{1,0:T(8,128)}, f32[192,384]{1,0:T(8,128)S(1)}, u32[]{:S(2)}) copy-start(f32[192,384]{1,0:T(8,128)S(1)} %get-tuple-element.134) | copy-start | bytes 884740
  59.8 21.2 %copy-start.2 = (f32[16,24,384]{2,1,0:T(8,128)S(1)}, f32[16,24,384]{2,1,0:T(8,128)}, u32[]{:S(2)}) copy-start(f32[16,24,384]{2,1,0:T(8,128)} %param.10) | copy-start | bytes 1769476
  59.8 50.2 %all-to-all-start = ((f32[1,1,384,768]{3,1,0,2:T(1,128)}), f32[1,1,384,768]{3,1,0,2:T(1,128)S(1)}, u32[]{:S(2)}, u32[]{:S(2)}) async-start(f32[1,1,384,768]{3,1,0,2:T(1,128)} %copy.112), calls=%async_computation | async-start | bytes 2359296 | tf_op jit(solution)/shard_map/all_to_all | solution.py:138
  117.6 34.2 %all-to-all-start.1 = ((f32[1,16,24,768]{3,2,0,1:T(8,128)}), f32[1,16,24,768]{3,2,0,1:T(8,128)S(1)}, u32[]{:S(2)}, u32[]{:S(2)}) async-start(f32[1,16,24,768]{3,2,0,1:T(8,128)} %copy.116), calls=%async_computation.1 | async-start | bytes 2359296 | tf_op jit(solution)/shard_map/all_to_all | solution.py:144
  122.8 185.3 %all-reduce.9.cloned.1.call-start = ((), (), s32[]{:S(2)}) async-start(), calls=%async_computation.4 | async-start | bytes 589824
  156.5 1.0 copy-start.3
  160.1 383.8 %copy-start.6 = (f32[192,384]{1,0:T(8,128)S(1)}, f32[192,384]{1,0:T(8,128)}, u32[]{:S(2)}) copy-start(f32[192,384]{1,0:T(8,128)} %copy-done.5) | copy-start | bytes 884740
  160.1 383.8 %copy-start.8 = (f32[192,384]{1,0:T(8,128)S(1)}, f32[192,384]{1,0:T(8,128)}, u32[]{:S(2)}) copy-start(f32[192,384]{1,0:T(8,128)} %copy-done.7) | copy-start | bytes 884740
  160.2 383.8 %copy-start.10 = (f32[192,384]{1,0:T(8,128)S(1)}, f32[192,384]{1,0:T(8,128)}, u32[]{:S(2)}) copy-start(f32[192,384]{1,0:T(8,128)} %copy-done.9) | copy-start | bytes 884740
  160.2 641.0 %all-reduce.11.cloned.1.call-start = ((), (), s32[]{:S(2)}) async-start(), calls=%async_computation.5 | async-start | bytes 589824
  648.8 1.0 copy-start.4
  903.1 7.1 collective-permute-start
  908.2 7.5 collective-permute-start.1
  915.8 7.5 collective-permute-start.3
  919.8 4.0 collective-permute-start.2
  936.2 0.8 copy-start.12
  938.3 5.3 collective-permute-start.4
  940.3 6.9 collective-permute-start.5
  947.4 9.9 collective-permute-start.7
  951.4 7.1 collective-permute-start.6
  975.2 2.9 copy-start.1
  980.2 5.3 collective-permute-start.8
  982.1 7.4 collective-permute-start.9
  989.6 9.7 collective-permute-start.11
  992.3 8.1 collective-permute-start.10
  1016.2 2.9 copy-start.11
Sparse Core Ops, SparseCore 0:
  160.3 147.8 all-reduce.8
  652.5 148.5 all-reduce.10
where the time goes:
time: 1030 us
  blocking collectives  449 us (44%)
  waiting for transfers between devices  362 us (35%)
  starting transfers between devices  68.6 us (7%)
  local copies, waits for them, and re-layouts  64.6 us (6%)
  matrix products  52.4 us (5%)
  between operations  19.8 us (2%)
  other arithmetic  12 us (1%)
    unnamed x4, waiting for transfers between devices  295 us
    psum x2, blocking collectives, total_squares(): return lax.psum(jnp.sum(residual * residual), ('coil', 'slab'))  194 us
    psum x1, blocking collectives, shards(): curvature = lax.psum(local_curv, ('coil', 'slab'))  98.9 us
    all_gather x2, blocking collectives, shards(): lax.all_gather(direction, 'coil', axis=1, tiled=True)[None]  74.3 us
    all_to_all x1, blocking collectives, shards(): lax.all_to_all(spread, 'slab', split_axis=2, concat_axis=1, tiled=True)  47.3 us
    all_to_all x1, blocking collectives, shards(): lax.all_to_all(returned, 'slab', split_axis=1, concat_axis=2, tiled=True)  34.2 us
    concatenate x12, local copies, waits for them, and re-layouts, convolve(): patches = jnp.concatenate(tap_list, axis=-1).reshape(-1, width_taps)  26.8 us
    all_to_all x1, waiting for transfers between devices, shards(): lax.all_to_all(spread, 'slab', split_axis=2, concat_axis=1, tiled=True)  25 us
  transfers between devices with their start and end apart: 16, of which 12 were waited for; matrix products, arithmetic and copies ran while one was open for 1% of the time, Pallas kernels for 0%

commit v1 on v0

--- a/solution.py
+++ b/solution.py
@@ -135,7 +135,12 @@
         )
         products = jnp.matmul(products, fwd_last, precision=highest)
         spread = along_axis(products, fwd_plane, "kn,cznw->czkw")
-        apply_pencil = lax.all_to_all(spread, "slab", split_axis=2, concat_axis=1, tiled=True)
+        apply_pencil = jnp.concatenate(
+            lax.all_to_all(
+                jnp.stack(jnp.split(spread, lax.axis_size("slab"), axis=2)), "slab", 0, 0
+            ),
+            axis=1,
+        )
         spectrum = along_axis(apply_pencil, fwd_depth, "kn,cnxw->ckxw")
         shape_now = spectrum.shape
         split_form = spectrum.reshape(shape_now[0], shape_now[1], shape_now[2], 2, grid_len)

time: 1030 us -> 1080 us (1.049)
  local copies, waits for them, and re-layouts: 64.6 us -> 106 us
    another operation x0 -> x34, local copies, waits for them, and re-layouts: none -> 36.5 us  [shards(): jnp.stack(jnp.split(spread, lax.axis_size('slab'), axis=2))]
    unnamed x36 -> x132, local copies, waits for them, and re-layouts: 6.16 us -> 17.3 us
where the time goes in v1:
time: 1080 us
  blocking collectives  448 us (41%)
  waiting for transfers between devices  362 us (34%)
  local copies, waits for them, and re-layouts  106 us (10%)
  starting transfers between devices  68.1 us (6%)
  matrix products  52.7 us (5%)
  between operations  20.1 us (2%)
  other arithmetic  20 us (2%)
    unnamed x4, waiting for transfers between devices  295 us
    psum x2, blocking collectives, total_squares(): return lax.psum(jnp.sum(residual * residual), ('coil', 'slab'))  194 us
    psum x1, blocking collectives, shards(): curvature = lax.psum(local_curv, ('coil', 'slab'))  99 us
    all_gather x2, blocking collectives, shards(): lax.all_gather(direction, 'coil', axis=1, tiled=True)[None]  74.3 us
    all_to_all x1, blocking collectives, shards(): lax.all_to_all(jnp.stack(jnp.split(spread, lax.axis_size('slab'), axis=2)...  46.5 us
    another operation x34, local copies, waits for them, and re-layouts, shards(): jnp.stack(jnp.split(spread, lax.axis_size('slab'), axis=2))  36.5 us
    all_to_all x1, blocking collectives, shards(): lax.all_to_all(returned, 'slab', split_axis=1, concat_axis=2, tiled=True)  34.4 us
    concatenate x12, local copies, waits for them, and re-layouts, convolve(): patches = jnp.concatenate(tap_list, axis=-1).reshape(-1, width_taps)  26.1 us
  transfers between devices with their start and end apart: 16, of which 12 were waited for; matrix products, arithmetic and copies ran while one was open for 1% of the time, Pallas kernels for 0%

profile of v1, /device:TPU:249, one launch (start us, length us, event | category | flops | bytes accessed | tf_op | source)
XLA Modules:
  0.0 1077.3 jit_solution(4605016260307838351)
XLA Ops:
  10.4 37.1 %all_gather.6 = f32[1,192,384]{2,0,1:T(1,128)S(1)} all-gather(f32[1,6,384]{2,0,1:T(1,128)S(1)} %copy.135), channel_id=1, replica_groups=mesh['coil'=32,'slab'=16] {'coil'}, dimensions={1}, use_global_device_ids=true | all-gather | bytes 304128 | tf_op jit(solution)/shard_map/all_gather | solution.py:134
  48.9 4.0 convolution_bitcast_fusion.10
  52.9 4.0 convolution_bitcast_fusion.11
  57.0 2.3 fusion.55
  86.8 20.6 %all-to-all-start = ((f32[16,1,1,24,768]{4,3,2,1,0:T(8,128)}), f32[16,1,1,24,768]{4,3,2,1,0:T(8,128)S(1)}, u32[]{:S(2)}, u32[]{:S(2)}) async-start(f32[16,1,1,24,768]{4,3,2,1,0:T(8,128)} %constant_dynamic-update-slice_fusion), calls=%async_computation | async-start | bytes 2359296 | tf_op jit(solution)/shard_map/all_to_all | solution.py:139
  109.2 2.2 mul.250
  111.5 25.0 %all-to-all-done = f32[16,1,1,24,768]{4,3,2,1,0:T(8,128)S(1)} async-done(((f32[16,1,1,24,768]{4,3,2,1,0:T(8,128)}), f32[16,1,1,24,768]{4,3,2,1,0:T(8,128)S(1)}, u32[]{:S(2)}, u32[]{:S(2)}) %all-to-all-start) | async-done | bytes 1179680 | tf_op jit(solution)/shard_map/all_to_all | solution.py:139
  143.9 5.2 all-to-all-start.1
  150.9 2.4 fusion.91
  153.3 24.8 %all-to-all-done.1 = f32[1,16,24,768]{3,2,0,1:T(8,128)S(1)} async-done(((f32[1,16,24,768]{3,2,0,1:T(8,128)}), f32[1,16,24,768]{3,2,0,1:T(8,128)S(1)}, u32[]{:S(2)}, u32[]{:S(2)}) %all-to-all-start.1) | async-done | bytes 1179680 | tf_op jit(solution)/shard_map/all_to_all | solution.py:149
  178.2 2.3 convolution_bitcast_fusion.14
  180.5 2.3 convolution_bitcast_fusion.15
  188.6 145.9 %all-reduce.9.cloned.1.call-done = f32[1,192,384]{2,0,1:T(1,128)} async-done(((f32[1,192,384]{2,0,1:T(1,128)}), f32[1,192,384]{2,0,1:T(1,128)}) %all-reduce.9.cloned.1.call-update) | async-done | bytes 294928
  335.8 99.0 %all-reduce.5 = (f32[]{:T(128)}, f32[]{:T(128)}) all-reduce(f32[]{:T(128)} %get-tuple-element.13, f32[]{:T(128)} %get-tuple-element.12), channel_id=1, replica_groups=mesh['coil'=32,'slab'=16] {'coil','slab'}, use_global_device_ids=true, to_apply=%region_1.2 | all-reduce | flops 2 | bytes 16 | tf_op jit(solution)/shard_map/psum | solution.py:125
  436.8 94.7 %psum.30 = f32[]{:T(128)} all-reduce(f32[]{:T(128)} %multiply_reduce_fusion), channel_id=1, replica_groups=mesh['coil'=32,'slab'=16] {'coil','slab'}, use_global_device_ids=true, to_apply=%region_6.7 | all-reduce | flops 1 | bytes 8 | tf_op jit(solution)/shard_map/psum | solution.py:125
  532.9 37.2 %all_gather.7 = f32[1,192,384]{2,0,1:T(1,128)S(1)} all-gather(f32[1,6,384]{2,0,1:T(1,128)S(1)} %copy.157), channel_id=1, replica_groups=mesh['coil'=32,'slab'=16] {'coil'}, dimensions={1}, use_global_device_ids=true | all-gather | bytes 304128 | tf_op jit(solution)/shard_map/all_gather | solution.py:134
  571.5 4.0 convolution_bitcast_fusion.8
  575.5 4.0 convolution_bitcast_fusion.9
  579.6 2.3 fusion.25
  581.9 2.0 fusion.84
  605.4 46.5 %all_to_all.28 = f32[16,1,1,24,768]{4,3,2,1,0:T(8,128)S(1)} all-to-all(f32[16,1,1,24,768]{4,3,2,1,0:T(8,128)S(1)} %constant_dynamic-update-slice_fusion.16), channel_id=1, replica_groups=mesh['coil'=32,'slab'=16] {'slab'}, dimensions={0} | all-to-all | bytes 2359296 | tf_op jit(solution)/shard_map/all_to_all | solution.py:139
  658.3 34.4 %all_to_all.29 = f32[1,16,24,768]{3,2,0,1:T(8,128)S(1)} all-to-all(f32[1,16,24,768]{3,2,0,1:T(8,128)S(1)} %copy.175), channel_id=1, replica_groups=mesh['coil'=32,'slab'=16] {'slab'}, dimensions={1} | all-to-all | bytes 2359296 | tf_op jit(solution)/shard_map/all_to_all | solution.py:149
  692.8 2.3 convolution_bitcast_fusion.12
  695.1 2.3 convolution_bitcast_fusion.13
  701.4 148.8 %all-reduce.11.cloned.1.call-done = f32[1,192,384]{2,0,1:T(1,128)} async-done(((f32[1,192,384]{2,0,1:T(1,128)}), f32[1,192,384]{2,0,1:T(1,128)}) %all-reduce.11.cloned.1.call-update) | async-done | bytes 294928
  851.4 99.0 %psum.31 = f32[]{:T(128)} all-reduce(f32[]{:T(128)} %fusion.140), channel_id=1, replica_groups=mesh['coil'=32,'slab'=16] {'coil','slab'}, use_global_device_ids=true, to_apply=%region_9.10 | all-reduce | flops 1 | bytes 8 | tf_op jit(solution)/shard_map/psum | solution.py:157
  952.1 5.1 collective-permute-start
  959.3 5.3 collective-permute-done.1
  964.8 4.0 collective-permute-start.3
  968.8 3.5 collective-permute-start.2
  976.2 4.2 concatenate.143
  989.5 3.4 collective-permute-start.5
  992.9 3.6 collective-permute-done.5
  996.6 4.0 collective-permute-start.7
  1000.7 4.7 collective-permute-start.6
  1012.1 2.0 pad_slice_fusion.79
  1014.1 3.1 concatenate.146
  1017.2 2.2 fusion.137
  1019.4 2.7 concatenate.147
  1022.1 2.5 convolution_add_fusion.1
  1024.7 2.6 concatenate.148
  1031.3 3.4 collective-permute-start.9
  1034.7 4.0 collective-permute-done.9
  1038.8 2.7 collective-permute-start.11
  1041.6 5.5 collective-permute-start.10
  1056.1 3.1 concatenate.151
  1060.9 2.7 concatenate.152
  1065.7 2.6 concatenate.153
  (274 shorter events, 125.8 us)
Async XLA Ops:
  7.2 40.4 %copy-start = (f32[1,1,192,384]{3,2,1,0:T(8,128)S(1)}, f32[1,1,192,384]{3,2,1,0:T(8,128)}, u32[]{:S(2)}) copy-start(f32[1,1,192,384]{3,2,1,0:T(8,128)} %param.9) | copy-start | bytes 884740
  8.3 39.4 %copy-start.40 = (f32[192,384]{1,0:T(8,128)}, f32[192,384]{1,0:T(8,128)S(1)}, u32[]{:S(2)}) copy-start(f32[192,384]{1,0:T(8,128)S(1)} %fusion.132) | copy-start | bytes 884740
  9.5 39.4 %copy-start.42 = (f32[192,384]{1,0:T(8,128)}, f32[192,384]{1,0:T(8,128)S(1)}, u32[]{:S(2)}) copy-start(f32[192,384]{1,0:T(8,128)S(1)} %get-tuple-element.165) | copy-start | bytes 884740
  9.5 39.4 %copy-start.44 = (f32[192,384]{1,0:T(8,128)}, f32[192,384]{1,0:T(8,128)S(1)}, u32[]{:S(2)}) copy-start(f32[192,384]{1,0:T(8,128)S(1)} %get-tuple-element.166) | copy-start | bytes 884740
  75.4 1.2 copy-start.37
  76.2 5.5 copy-start.33
  76.4 6.0 copy-start.31
  76.4 6.6 copy-start.29
  76.4 7.3 copy-start.27
  76.5 7.8 copy-start.23
  76.5 8.4 copy-start.24
  76.7 9.5 copy-start.21
  86.8 20.6 %copy-start.11 = (f32[16,24,384]{2,1,0:T(8,128)S(1)}, f32[16,24,384]{2,1,0:T(8,128)}, u32[]{:S(2)}) copy-start(f32[16,24,384]{2,1,0:T(8,128)} %param.10) | copy-start | bytes 1769476
  86.8 49.6 %all-to-all-start = ((f32[16,1,1,24,768]{4,3,2,1,0:T(8,128)}), f32[16,1,1,24,768]{4,3,2,1,0:T(8,128)S(1)}, u32[]{:S(2)}, u32[]{:S(2)}) async-start(f32[16,1,1,24,768]{4,3,2,1,0:T(8,128)} %constant_dynamic-update-slice_fusion), calls=%async_computation | async-start | bytes 2359296 | tf_op jit(solution)/shard_map/all_to_all | solution.py:139
  143.9 34.2 %all-to-all-start.1 = ((f32[1,16,24,768]{3,2,0,1:T(8,128)}), f32[1,16,24,768]{3,2,0,1:T(8,128)S(1)}, u32[]{:S(2)}, u32[]{:S(2)}) async-start(f32[1,16,24,768]{3,2,0,1:T(8,128)} %copy.154), calls=%async_computation.1 | async-start | bytes 2359296 | tf_op jit(solution)/shard_map/all_to_all | solution.py:149
  149.2 185.4 %all-reduce.9.cloned.1.call-start = ((), (), s32[]{:S(2)}) async-start(), calls=%async_computation.4 | async-start | bytes 589824
  150.9 32.0 %copy-start.15 = (f32[384,192]{1,0:T(8,128)}, f32[384,192]{1,0:T(8,128)S(1)}, u32[]{:S(2)}) copy-start(f32[384,192]{1,0:T(8,128)S(1)} %fusion.125) | copy-start | bytes 884740
  153.3 29.6 %copy-start.17 = (f32[384,192]{1,0:T(8,128)}, f32[384,192]{1,0:T(8,128)S(1)}, u32[]{:S(2)}) copy-start(f32[384,192]{1,0:T(8,128)S(1)} %get-tuple-element.167) | copy-start | bytes 884740
  186.5 383.8 %copy-start.41 = (f32[192,384]{1,0:T(8,128)S(1)}, f32[192,384]{1,0:T(8,128)}, u32[]{:S(2)}) copy-start(f32[192,384]{1,0:T(8,128)} %copy-done.40) | copy-start | bytes 884740
  186.5 383.8 %copy-start.43 = (f32[192,384]{1,0:T(8,128)S(1)}, f32[192,384]{1,0:T(8,128)}, u32[]{:S(2)}) copy-start(f32[192,384]{1,0:T(8,128)} %copy-done.42) | copy-start | bytes 884740
  186.5 383.8 %copy-start.45 = (f32[192,384]{1,0:T(8,128)S(1)}, f32[192,384]{1,0:T(8,128)}, u32[]{:S(2)}) copy-start(f32[192,384]{1,0:T(8,128)} %copy-done.44) | copy-start | bytes 884740
  186.5 663.6 %all-reduce.11.cloned.1.call-start = ((), (), s32[]{:S(2)}) async-start(), calls=%async_computation.5 | async-start | bytes 589824
  604.2 1.0 copy-start.28
  697.5 1.0 copy-start.16
  697.5 1.1 copy-start.18
  697.5 1.2 copy-start.20
  952.1 7.1 collective-permute-start
  957.2 7.5 collective-permute-start.1
  964.8 7.5 collective-permute-start.3
  968.8 4.0 collective-permute-start.2
  987.6 5.3 collective-permute-start.4
  989.5 6.9 collective-permute-start.5
  996.6 9.9 collective-permute-start.7
  1000.7 7.1 collective-permute-start.6
  1022.1 2.5 copy-start.1
  1022.1 2.5 copy-start.2
  1022.1 2.5 copy-start.3
  1022.1 2.5 copy-start.4
  1022.1 2.5 copy-start.5
  1029.4 5.3 collective-permute-start.8
  1031.3 7.4 collective-permute-start.9
  1038.8 9.7 collective-permute-start.11
  1041.6 8.1 collective-permute-start.10
  1063.6 2.0 copy-start.6
  1063.6 2.0 copy-start.7
  1063.6 2.0 copy-start.8
  1063.7 2.0 copy-start.9
  1063.7 2.0 copy-start.10
  (15 other events, 14.1 us)
Sparse Core Ops, SparseCore 0:
  186.6 147.8 all-reduce.8
  701.5 148.6 all-reduce.10
